TPU v7x, 32 devices: a whole 2x2x4 slice. The times are simulated.
32 devices in a mesh: groups: 2 (over y), vocab: 4 (over z), tokens: 2 (over x), section: 2 (over core).
Axes of the slice: x: 2, y: 2, z: 4, core: 2. Of those that a mesh axis runs over, the one named last changes fastest.
Arguments:
- teacher_hidden: bfloat16 [512, 16384], P(('groups', 'vocab', 'section'), 'tokens'), parts along dimension 0
- teacher_weight: bfloat16 [16384, 4096], P('tokens', ('vocab', 'section'))
- student_hidden: bfloat16 [512, 4096], P(('groups', 'tokens')), parts along dimension 0
- student_gain: float32 [4096], replicated, may hold values from 0.5 to 1.5
- student_weight: bfloat16 [4096, 4096], P('tokens', ('vocab', 'section'))
- labels: int32 [512], P(('groups', 'tokens')), parts along dimension 0, may hold values from 0 to 4095
- alignment: int32 [512], P(('groups', 'tokens')), parts along dimension 0, may hold values from 0 to 255, as said below
- loss_mask: int32 [512], P('groups'), parts along dimension 0, may hold values from 0 to 1, as said below
Outputs:
- row_loss: float32 [512], P(('groups', 'tokens')), parts along dimension 0
- logit_grad: bfloat16 [512, 4096], P(('groups', 'tokens'), ('vocab', 'section')), parts along dimension 0
- hidden_grad: bfloat16 [512, 4096], P(('groups', 'tokens'), ('vocab', 'section')), parts along dimension 0
There are 2 independent parts, one for each index of `groups`. A program takes and returns all parts, laid end to end along the dimension named above; an argument that names none is the same for every part. Nothing has to cross between parts.
Inputs may be any that keep to these rules, and one draw needn't show every extreme that they name: Within each aligned block of 128 frames the alignment never falls, names only tokens of the same block, and starts at the block's first token and ends at its last. `loss_mask`: the last frame always counts.
All inputs are finite; a program needn't handle non-finite values.
Results may differ from a plain program's by a relative error of at most 0.0061.
Values may be sent and summed in bfloat16 or wider, within the bound.
A program may use at most 64 MiB of HBM per device.

v0:
```python
import jax
import jax.numpy as jnp
from jax import lax
from jax.sharding import PartitionSpec as P

label_weight = 0.2
loss_scale = 16.0
epsilon = 1e-05


def merged(shard, axis, combine):
    everything = jax.tree.map(lambda part: lax.all_gather(part, axis), shard)
    leading = jax.tree.map(lambda part: part[0], everything)

    def hop(k, so_far):
        return combine(so_far, jax.tree.map(lambda part: part[k], everything))

    return lax.fori_loop(1, lax.axis_size(axis), hop, leading)


def merge_rows(former, latter):
    top_t = jnp.maximum(former[0], latter[0])
    left_t = jnp.exp(former[0] - top_t)
    right_t = jnp.exp(latter[0] - top_t)
    top_s = jnp.maximum(former[3], latter[3])
    left_s = jnp.exp(former[3] - top_s)
    right_s = jnp.exp(latter[3] - top_s)
    return (
        top_t,
        former[1] * left_t + latter[1] * right_t,
        former[2] * left_t + latter[2] * right_t,
        top_s,
        former[4] * left_s + latter[4] * right_s,
        former[5] + latter[5],
    )


def local(
    teacher_hidden,
    teacher_weight,
    student_hidden,
    student_gain,
    student_weight,
    labels,
    alignment,
    loss_mask,
):
    frames = student_hidden.shape[0]
    columns = teacher_weight.shape[1]
    partial_rows = jnp.dot(
        lax.all_gather(teacher_hidden, ("vocab", "section"), axis=0, tiled=True),
        teacher_weight,
        preferred_element_type=jnp.float32,
    )
    block_logits = lax.psum_scatter(partial_rows, "tokens", scatter_dimension=0, tiled=True)
    block_start = lax.axis_index("tokens") * frames
    local_index = alignment - block_start
    aligned = jnp.take(block_logits, local_index, axis=0)
    hidden = student_hidden.astype(jnp.float32)
    inverse = lax.rsqrt(jnp.mean(hidden * hidden, axis=1, keepdims=True) + epsilon)
    normed = (hidden * inverse * student_gain).astype(jnp.bfloat16)
    full_weight = lax.all_gather(student_weight, "tokens", axis=0, tiled=True)
    student = jnp.dot(normed, full_weight, preferred_element_type=jnp.float32)
    column_start = lax.axis_index(("vocab", "section")) * columns
    onehot = labels[:, None] - column_start == jnp.arange(columns, dtype=jnp.int32)[None, :]
    label_logit = jnp.sum(jnp.where(onehot, student, 0.0), axis=1)
    top_t = jnp.max(aligned, axis=1)
    top_s = jnp.max(student, axis=1)
    exp_t = jnp.exp(aligned - top_t[:, None])
    exp_s = jnp.exp(student - top_s[:, None])
    local_stats = (
        top_t,
        jnp.sum(exp_t, axis=1),
        jnp.sum(exp_t * (aligned - student), axis=1),
        top_s,
        jnp.sum(exp_s, axis=1),
        label_logit,
    )
    top_t, sum_t, cross_t, top_s, sum_s, label_logit = merged(
        local_stats, ("vocab", "section"), merge_rows
    )
    lse_t = top_t + jnp.log(sum_t)
    lse_s = top_s + jnp.log(sum_s)
    diverge = cross_t / sum_t - lse_t + lse_s
    cross_term = lse_s - label_logit
    mask_float = loss_mask.astype(jnp.float32)
    mask_count = jnp.sum(mask_float)
    own_mask = lax.dynamic_slice_in_dim(mask_float, block_start, frames, 0)
    row_weight = own_mask * loss_mask.shape[0] / mask_count
    row_loss = row_weight * (diverge + label_weight * cross_term)
    teacher_prob = jnp.exp(aligned - lse_t[:, None])
    student_prob = jnp.exp(student - lse_s[:, None])
    onehot_float = onehot.astype(jnp.float32)
    logit_grad = (
        loss_scale
        * row_weight[:, None]
        * ((1.0 + label_weight) * student_prob - teacher_prob - label_weight * onehot_float)
    ).astype(jnp.bfloat16)
    normed_grad = lax.dot_general(
        logit_grad, full_weight, (((1,), (1,)), ((), ())), preferred_element_type=jnp.float32
    )
    share_width = student_gain.shape[0] // lax.axis_size(("vocab", "section"))
    part_start = lax.axis_index(("vocab", "section")) * share_width
    grad_total = lax.psum(normed_grad, ("vocab", "section"))
    scaled = grad_total * student_gain
    inner_rows = jnp.sum(scaled * hidden, axis=1, keepdims=True)
    result = inverse * scaled - hidden * inverse**3 * inner_rows / hidden.shape[1]
    hidden_grad = lax.dynamic_slice_in_dim(result, part_start, share_width, 1).astype(jnp.bfloat16)
    return (row_loss, logit_grad, hidden_grad)


def solution(mesh):
    in_specs = (
        P(("groups", "vocab", "section"), "tokens"),
        P("tokens", ("vocab", "section")),
        P(("groups", "tokens"), None),
        P(),
        P("tokens", ("vocab", "section")),
        P(("groups", "tokens")),
        P(("groups", "tokens")),
        P("groups"),
    )
    out_specs = (
        P(("groups", "tokens")),
        P(("groups", "tokens"), ("vocab", "section")),
        P(("groups", "tokens"), ("vocab", "section")),
    )
    return jax.shard_map(local, mesh=mesh, in_specs=in_specs, out_specs=out_specs, check_vma=False)
```

profile of v0, /device:TPU:0, one launch (start us, length us, event | category | flops | bytes accessed | tf_op | source)
XLA Modules:
  0.0 262.9 jit_solution(11677648627464379250)
XLA Ops:
  7.2 0.7 all-gather.15.cloned.1.call-update
  8.0 0.7 all-gather.17.cloned.1.call-update
  8.8 0.6 convert_reduce_fusion
  9.4 0.7 broadcast_multiply_fusion.1
  10.1 0.3 multiply_reduce_fusion.1
  10.4 49.1 %all-gather.15.cloned.1.call-done = bf16[256,8192]{1,0:T(8,128)(2,1)} async-done(((bf16[32,8192]{1,0:T(8,128)(2,1)}), bf16[256,8192]{1,0:T(8,128)(2,1)}) %all-gather.15.cloned.1.call-update) | async-done | bytes 4194320 | tf_op jit(solution)/shard_map/all_gather | solution.py:51
  59.5 7.8 %fusion.26 = f32[256,512]{1,0:T(8,128)} fusion(bf16[256,8192]{1,0:T(8,128)(2,1)} %all-gather.15.cloned.1.call-done, bf16[8192,512]{1,0:T(8,128)(2,1)} %param.11), kind=kOutput, calls=%fused_computation.64 | convolution fusion | flops 2147483648 | bytes 13107200 | tf_op jit(solution)/shard_map/dot_general | solution.py:50
  67.4 49.1 %all-gather.17.cloned.1.call-done = bf16[4096,512]{1,0:T(8,128)(2,1)} async-done(((bf16[2048,512]{1,0:T(8,128)(2,1)}), bf16[4096,512]{1,0:T(8,128)(2,1)}) %all-gather.17.cloned.1.call-update) | async-done | bytes 4194320 | tf_op jit(solution)/shard_map/all_gather | solution.py:62
  116.6 3.0 %fusion.25 = (f32[128]{0:T(128)S(1)}, f32[128,512]{1,0:T(8,128)S(1)}) fusion(bf16[4096,512]{1,0:T(8,128)(2,1)} %all-gather.17.cloned.1.call-done, bf16[128,4096]{1,0:T(8,128)(2,1)S(1)} %copy-done, f32[4096]{0:T(1024)S(1)} %copy-done.2, f32[128]{0:T(128)S(1)} %get-tuple-element.369), kind=kOutput, calls=%fused_computation.63 | convolution fusion | flops 539033472 | bytes 5522432 | tf_op jit(solution)/shard_map/dot_general | solution.py:63
  119.6 11.7 %all-gather.9 = f32[8,1,128]{2,1,0:T(1,128)S(1)} all-gather(f32[1,1,128]{2,1,0:T(1,128)S(1)} %bitcast.80), channel_id=5, replica_groups=mesh['groups'=2,'vocab'=4,'tokens'=2,'section'=2] {'vocab','section'}, dimensions={0}, use_global_device_ids=true | all-gather | bytes 4608 | tf_op jit(solution)/shard_map/all_gather | solution.py:12
  131.2 2.2 reduce-scatter.2.cloned.1.call-done
  133.4 1.8 gather_fusion
  135.4 11.7 %all-gather.6 = f32[8,1,128]{2,1,0:T(1,128)S(1)} all-gather(f32[1,1,128]{2,1,0:T(1,128)S(1)} %bitcast.79), channel_id=2, replica_groups=mesh['groups'=2,'vocab'=4,'tokens'=2,'section'=2] {'vocab','section'}, dimensions={0}, use_global_device_ids=true | all-gather | bytes 4608 | tf_op jit(solution)/shard_map/all_gather | solution.py:12
  147.1 0.3 select_reduce_fusion
  147.4 8.6 %all-gather.10 = f32[8,1,128]{2,1,0:T(1,128)S(1)} all-gather(f32[1,1,128]{2,1,0:T(1,128)S(1)} %bitcast.84), channel_id=6, replica_groups=mesh['groups'=2,'vocab'=4,'tokens'=2,'section'=2] {'vocab','section'}, dimensions={0}, use_global_device_ids=true | all-gather | bytes 4608 | tf_op jit(solution)/shard_map/all_gather | solution.py:12
  156.0 10.0 %all-gather.11 = f32[8,1,128]{2,1,0:T(1,128)S(1)} all-gather(f32[1,1,128]{2,1,0:T(1,128)S(1)} %bitcast.83), channel_id=7, replica_groups=mesh['groups'=2,'vocab'=4,'tokens'=2,'section'=2] {'vocab','section'}, dimensions={0}, use_global_device_ids=true | all-gather | bytes 4608 | tf_op jit(solution)/shard_map/all_gather | solution.py:12
  166.0 8.6 %all-gather.7 = f32[8,1,128]{2,1,0:T(1,128)S(1)} all-gather(f32[1,1,128]{2,1,0:T(1,128)S(1)} %bitcast.82), channel_id=3, replica_groups=mesh['groups'=2,'vocab'=4,'tokens'=2,'section'=2] {'vocab','section'}, dimensions={0}, use_global_device_ids=true | all-gather | bytes 4608 | tf_op jit(solution)/shard_map/all_gather | solution.py:12
  174.7 10.0 %all-gather.8 = f32[8,1,128]{2,1,0:T(1,128)S(1)} all-gather(f32[1,1,128]{2,1,0:T(1,128)S(1)} %bitcast.81), channel_id=4, replica_groups=mesh['groups'=2,'vocab'=4,'tokens'=2,'section'=2] {'vocab','section'}, dimensions={0}, use_global_device_ids=true | all-gather | bytes 4608 | tf_op jit(solution)/shard_map/all_gather | solution.py:12
  184.7 0.7 while.25
  185.4 0.5 add_multiply_fusion
  186.2 5.0 %fusion.27 = f32[128,4096]{1,0:T(8,128)} fusion(bf16[128,512]{1,0:T(8,128)(2,1)S(1)} %multiply_convert_fusion.2, bf16[4096,512]{1,0:T(8,128)(2,1)} %all-gather.17.cloned.1.call-done), kind=kOutput, calls=%fused_computation.65 | convolution fusion | flops 536870912 | bytes 6422528 | tf_op jit(solution)/shard_map/dot_general | solution.py:99
  191.4 62.1 %all-reduce.2.cloned.1.call-done = f32[128,4096]{1,0:T(8,128)} async-done(((f32[128,4096]{1,0:T(8,128)}), f32[128,4096]{1,0:T(8,128)}) %all-reduce.2.cloned.1.call-update) | async-done | bytes 2097168 | tf_op jit(solution)/shard_map/psum | solution.py:104
  253.6 2.0 multiply_reduce_fusion
  255.5 0.8 fusion.19
  (60 shorter events, 1.4 us)
Async XLA Ops:
  7.2 1.6 copy-start.3
  7.2 2.9 %copy-start.4 = (s32[128]{0:T(128)S(1)}, s32[128]{0:T(128)}, u32[]{:S(2)}) copy-start(s32[128]{0:T(128)} %param.16) | copy-start | bytes 1540
  7.2 2.9 %copy-start = (bf16[128,4096]{1,0:T(8,128)(2,1)S(1)}, bf16[128,4096]{1,0:T(8,128)(2,1)}, u32[]{:S(2)}) copy-start(bf16[128,4096]{1,0:T(8,128)(2,1)} %param.12) | copy-start | bytes 3145732
  7.2 52.3 %all-gather.15.cloned.1.call-start = ((), (), s32[]{:S(2)}) async-start(), calls=%async_computation.1 | async-start | bytes 4718592 | tf_op jit(solution)/shard_map/all_gather | solution.py:51
  7.9 108.6 %all-gather.17.cloned.1.call-start = ((), (), s32[]{:S(2)}) async-start(), calls=%async_computation.3 | async-start | bytes 6291456 | tf_op jit(solution)/shard_map/all_gather | solution.py:62
  8.7 124.7 %reduce-scatter.2.cloned.1.call-start = ((), (), s32[]{:S(2)}) async-start(), calls=%async_computation.2 | async-start | bytes 786432 | tf_op jit(solution)/shard_map/reduce_scatter | solution.py:55
  10.4 57.0 %copy-start.5 = (s32[128]{0:T(128)S(1)}, s32[128]{0:T(128)}, u32[]{:S(2)}) copy-start(s32[128]{0:T(128)} %param.15) | copy-start | bytes 1540
  10.4 106.1 %copy-start.2 = (f32[4096]{0:T(1024)S(1)}, f32[4096]{0:T(1024)}, u32[]{:S(2)}) copy-start(f32[4096]{0:T(1024)} %param.13) | copy-start | bytes 49156
  67.4 186.2 %all-reduce.2.cloned.1.call-start = ((), (), s32[]{:S(2)}) async-start(), calls=%async_computation.4 | async-start | bytes 4194304 | tf_op jit(solution)/shard_map/psum | solution.py:104
  186.2 5.0 %copy-start.1 = (bf16[128,512]{1,0:T(8,128)(2,1)}, bf16[128,512]{1,0:T(8,128)(2,1)S(1)}, u32[]{:S(2)}) copy-start(bf16[128,512]{1,0:T(8,128)(2,1)S(1)} %multiply_convert_fusion.2) | copy-start | bytes 393220
Sparse Core Ops, SparseCore 0:
  9.6 49.8 all-gather.14
  61.1 55.4 all-gather.16
  118.8 14.5 reduce-scatter.1
  191.3 62.1 all-reduce.1
where the time goes:
time: 263 us
  waiting for transfers between devices  164 us (62%)
  blocking collectives  60.6 us (23%)
  matrix products  15.9 us (6%)
  between operations  13.9 us (5%)
  other arithmetic  6.31 us (2%)
    psum x1, waiting for transfers between devices, local(): grad_total = lax.psum(normed_grad, ('vocab', 'section'))  62.1 us
    all_gather x6, blocking collectives, merged(): everything = jax.tree.map(lambda part: lax.all_gather(part, axis), shard)  60.6 us
    all_gather x1, waiting for transfers between devices, local(): full_weight = lax.all_gather(student_weight, 'tokens', axis=0, tiled=True)  49.1 us
    all_gather x1, waiting for transfers between devices, local(): lax.all_gather(teacher_hidden, ('vocab', 'section'), axis=0, tiled=True)  49.1 us
    dot_general x1, matrix products, local(): jnp.dot(lax.all_gather(teacher_hidden, ('vocab', 'section'), axis=0, tile...  7.83 us
  transfers between devices with their start and end apart: 4, of which 4 were waited for; matrix products, arithmetic and copies ran while one was open for 5% of the time, Pallas kernels for 0%

commit v1 on v0

v1 whole, which is shorter than its diff:
```python
import functools

import jax
import jax.numpy as jnp
from jax import lax
from jax.experimental import pallas as pl
from jax.experimental.pallas import tpu as pltpu
from jax.sharding import PartitionSpec as P

label_weight = 0.2
loss_scale = 16.0
epsilon = 1e-05
MESH = pl.DeviceIdType.MESH


def kernel(
    sizes, th, tw, sh, gain, sw, labels, align, mask,
    rl_out, lg_out, hg_out,
    tbuf, twv, wbuf, normed, acc, tin, bl, stats, inner_in, sibout, sibin, part, rin, lin, inner_acc,
    tw_sem, own_sem, sw_sem,
    left_send, right_send, sib_send, z_recv, s_recv,
    x_send, x_recv, y_send, y_recv,
    acc_send, acc_recv,
    stat_send, stat_recv, inner_send, inner_recv,
    gs_send, gs_recv, ln_send, r_recv, l_recv,
):
    G, V, T, S, C, CW = sizes
    VS = V * S
    g, v, t, s = (lax.axis_index(a) for a in ("groups", "vocab", "tokens", "section"))
    me = v * S + s
    rows = th.shape[0]
    fc = th.shape[1] // C
    F = sw.shape[0]
    half = F // 2
    wc = half // CW
    frames, DS = sh.shape
    N = tw.shape[1]
    w = DS // VS
    per = V // T

    def did(gg=None, vv=None, tt=None, ss=None):
        pick = lambda a, b: b if a is None else a
        return (pick(gg, g), pick(vv, v), pick(tt, t), pick(ss, s))

    def remote(src, dst, send, recv, where):
        return pltpu.make_async_remote_copy(
            src_ref=src, dst_ref=dst, send_sem=send, recv_sem=recv,
            device_id=where, device_id_type=MESH,
        )

    def vs_peer(k):
        other = lax.rem(me + k, VS)
        return did(vv=other // S, ss=lax.rem(other, S)), other

    def each(lo, hi, body):
        def run(i, carry):
            body(i)
            return carry
        lax.fori_loop(lo, hi, run, 0)

    barrier = pltpu.get_barrier_semaphore()

    def greet(where):
        pl.semaphore_signal(barrier, inc=1, device_id=where, device_id_type=MESH)

    for c in range(C):
        pltpu.make_async_copy(tw.at[c * fc:(c + 1) * fc], twv.at[c], tw_sem.at[c]).start()
        pltpu.make_async_copy(th.at[:, c * fc:(c + 1) * fc], tbuf.at[c, me], own_sem.at[c]).start()
    sw_copy = pltpu.make_async_copy(sw, wbuf.at[pl.ds(pl.multiple_of(t * F, F), F)], sw_sem)
    sw_copy.start()

    each(1, VS, lambda k: greet(vs_peer(k)[0]))
    each(1, T, lambda k: greet(did(tt=lax.rem(t + k, T))))
    greet(did(gg=1 - g))
    pl.semaphore_wait(barrier, VS - 1 + T - 1 + 1)

    def go_left(o, c, src):
        return remote(src, tbuf.at[c, o * S + s], left_send.at[o, c], z_recv.at[o, c], did(vv=v - 1))

    def go_right(o, c, src):
        return remote(src, tbuf.at[c, o * S + s], right_send.at[o, c], z_recv.at[o, c], did(vv=v + 1))

    def go_sib(o, c, src):
        return remote(src, tbuf.at[c, o * S + s], sib_send.at[o, c], s_recv.at[o, c], did(ss=1 - s))

    for c in range(C):
        own = th.at[:, c * fc:(c + 1) * fc]

        @pl.when(v > 0)
        def _():
            go_left(v, c, own).start()

        @pl.when(v < V - 1)
        def _():
            go_right(v, c, own).start()

    def w_at(tt, hh, cw):
        return wbuf.at[pl.ds(pl.multiple_of(tt * F + hh * half + cw * wc, wc), wc)]

    def go_x(k, cw):
        to = lax.rem(t + k, T)
        src = sw.at[pl.ds(pl.multiple_of(g * half + cw * wc, wc), wc)]
        return remote(src, w_at(t, g, cw), x_send.at[to, cw], x_recv.at[t, cw], did(tt=to))

    def go_y(tt, cw):
        return remote(w_at(tt, g, cw), w_at(tt, g, cw), y_send.at[tt, cw], y_recv.at[tt, cw], did(gg=1 - g))

    def x_wait(tt, cw):
        remote(w_at(tt, g, cw), w_at(tt, g, cw), x_send.at[tt, cw], x_recv.at[tt, cw], did(tt=tt)).wait_recv()

    def y_wait(tt, cw):
        remote(w_at(tt, 1 - g, cw), w_at(tt, 1 - g, cw), y_send.at[tt, cw], y_recv.at[tt, cw], did(gg=1 - g)).wait_recv()

    nev = (T - 1) * CW
    each(0, nev, lambda j: go_x(j // CW + 1, lax.rem(j, CW)).start())
    for c in range(C):
        go_sib(v, c, th.at[:, c * fc:(c + 1) * fc]).start()

    def pass_on(j):
        tt = lax.rem(t + T - 1 - j // CW, T)
        cw = lax.rem(j, CW)
        x_wait(tt, cw)
        go_y(tt, cw).start()

    hid = sh[...].astype(jnp.float32)
    inverse = lax.rsqrt(jnp.mean(hid * hid, axis=1, keepdims=True) + epsilon)
    normed[...] = (hid * inverse * gain[...]).astype(jnp.bfloat16)

    def multiply(o, c):
        x = tbuf[c, pl.ds(o * S, S)].reshape(S * rows, fc)
        acc[o] += jnp.dot(x, twv[c], preferred_element_type=jnp.float32)

    def go_acc(o):
        to = o // per
        return remote(acc.at[o], tin.at[t, lax.rem(o, per)], acc_send.at[o], acc_recv.at[t, lax.rem(o, per)], did(tt=to))

    def finished(o):
        @pl.when(o // per != t)
        def _():
            go_acc(o).start()

    acc[...] = jnp.zeros_like(acc)

    def own_chunk(c):
        pltpu.make_async_copy(tbuf.at[c, me], tbuf.at[c, me], own_sem.at[c]).wait()
        pltpu.make_async_copy(twv.at[c], twv.at[c], tw_sem.at[c]).wait()
        other = tbuf.at[c, v * S + 1 - s]
        remote(other, other, sib_send.at[v, c], s_recv.at[v, c], did(ss=1 - s)).wait_recv()
        multiply(v, c)

    each(0, C, own_chunk)
    finished(v)

    def take(o, c, onward, has_next):
        here = tbuf.at[c, o * S + s]
        remote(here, here, sib_send.at[o, c], z_recv.at[o, c], did(ss=1 - s)).wait_recv()

        @pl.when(has_next)
        def _():
            onward(o, c, here).start()

        go_sib(o, c, here).start()

    def use(o, c):
        other = tbuf.at[c, o * S + 1 - s]
        remote(other, other, sib_send.at[o, c], s_recv.at[o, c], did(ss=1 - s)).wait_recv()
        multiply(o, c)

        @pl.when(c == C - 1)
        def _():
            finished(o)

    steps = (V - 1) * C
    stride = max(1, (steps - 2) // nev)

    def step(i):
        k, c = i // C + 1, lax.rem(i, C)

        @pl.when(i < steps)
        def _():
            @pl.when(v + k < V)
            def _():
                take(v + k, c, go_left, v > 0)

            @pl.when(v - k >= 0)
            def _():
                take(v - k, c, go_right, v < V - 1)

        j = i // stride - 1

        @pl.when((lax.rem(i, stride) == 0) & (j >= 0) & (j < nev))
        def _():
            pass_on(j)

        @pl.when(i > 0)
        def _():
            kk, cc = (i - 1) // C + 1, lax.rem(i - 1, C)

            @pl.when(v + kk < V)
            def _():
                use(v + kk, cc)

            @pl.when(v - kk >= 0)
            def _():
                use(v - kk, cc)

    each(0, steps + 1, step)
    each(min(nev, steps // stride), nev, pass_on)

    sw_copy.wait()

    def y_in(j):
        y_wait(lax.rem(t + T - 1 - j // CW, T), lax.rem(j, CW))

    each(0, nev, y_in)
    student = jnp.dot(normed[...], wbuf[...], preferred_element_type=jnp.float32)
    lane_n = lax.broadcasted_iota(jnp.int32, (frames, N), 1)
    lane = lax.broadcasted_iota(jnp.int32, (frames, frames), 1)
    sub = lax.broadcasted_iota(jnp.int32, (frames, frames), 0)

    def to_columns(row):
        return jnp.transpose(jnp.broadcast_to(row, (frames, frames)))

    label_col = to_columns(labels[...].astype(jnp.float32)).astype(jnp.int32)[:, 0:1]
    onehot = (label_col - me * N) == lane_n
    label_logit = jnp.sum(jnp.where(onehot, student, 0.0), axis=1, keepdims=True)
    top_s = jnp.max(student, axis=1, keepdims=True)
    sum_s = jnp.sum(jnp.exp(student - top_s), axis=1, keepdims=True)
    align_cols = to_columns(align[...].astype(jnp.float32)).astype(jnp.int32) - t * frames
    pick = (align_cols == lane).astype(jnp.bfloat16)

    def tin_wait(j):
        tt, p = lax.rem(t + 1 + j // per, T), lax.rem(j, per)
        remote(tin.at[tt, p], tin.at[tt, p], acc_send.at[0], acc_recv.at[tt, p], did(tt=tt)).wait_recv()

    each(0, (T - 1) * per, tin_wait)
    for p in range(per):
        total = acc[t * per + p]
        for k in range(1, T):
            total = total + tin[lax.rem(t + k, T), p]
        bl[p * S * rows:(p + 1) * S * rows, :] = total
    whole = bl[...]
    hi = whole.astype(jnp.bfloat16)
    rest = whole - hi.astype(jnp.float32)
    mid = rest.astype(jnp.bfloat16)
    low = (rest - mid.astype(jnp.float32)).astype(jnp.bfloat16)
    rows_of = lambda piece: jnp.dot(pick, piece, preferred_element_type=jnp.float32)
    aligned = (rows_of(low) + rows_of(mid)) + rows_of(hi)
    top_t = jnp.max(aligned, axis=1, keepdims=True)
    exp_t = jnp.exp(aligned - top_t)
    sum_t = jnp.sum(exp_t, axis=1, keepdims=True)
    cross_t = jnp.sum(exp_t * (aligned - student), axis=1, keepdims=True)

    packed = jnp.zeros((frames, frames), jnp.float32)
    for i, column in enumerate((top_t, sum_t, cross_t, top_s, sum_s, label_logit)):
        packed = jnp.where(lane == i, column, packed)
    stats[me] = jnp.transpose(packed)[0:8, :]

    def go_stat(k):
        where, other = vs_peer(k)
        return remote(stats.at[me], stats.at[me], stat_send.at[other], stat_recv.at[me], where)

    each(1, VS, lambda k: go_stat(k).start())

    def stat_wait(k):
        where, other = vs_peer(k)
        remote(stats.at[other], stats.at[other], stat_send.at[other], stat_recv.at[other], where).wait_recv()

    each(1, VS, stat_wait)
    st = stats[...]
    row = lambda i: st[:, i, :]
    all_t = jnp.max(row(0), axis=0, keepdims=True)
    all_s = jnp.max(row(3), axis=0, keepdims=True)
    scale_t = jnp.exp(row(0) - all_t)
    scale_s = jnp.exp(row(3) - all_s)
    add = lambda x: jnp.sum(x, axis=0, keepdims=True)
    total_t = add(row(1) * scale_t)
    lse_t = all_t + jnp.log(total_t)
    lse_s = all_s + jnp.log(add(row(4) * scale_s))
    diverge = add(row(2) * scale_t) / total_t - lse_t + lse_s
    cross_term = lse_s - add(row(5))
    mask_float = mask[...].astype(jnp.float32)
    mask_count = jnp.sum(jnp.sum(mask_float, axis=1, keepdims=True), axis=0, keepdims=True)
    own_mask = mask[pl.ds(t, 1), :].astype(jnp.float32)
    row_weight = own_mask * (T * frames) / mask_count
    rl_out[...] = row_weight * (diverge + label_weight * cross_term)

    unpacked = jnp.where(sub == 0, lse_t, jnp.where(sub == 1, lse_s, row_weight))
    columns = jnp.transpose(unpacked)
    teacher_prob = jnp.exp(aligned - columns[:, 0:1])
    student_prob = jnp.exp(student - columns[:, 1:2])
    grad = (
        loss_scale * columns[:, 2:3]
        * ((1.0 + label_weight) * student_prob - teacher_prob - label_weight * onehot.astype(jnp.float32))
    ).astype(jnp.bfloat16)
    lg_out[...] = grad

    inner_acc[...] = jnp.zeros_like(inner_acc)

    def term(block):
        at = pl.multiple_of(block * w, w)
        value = lax.dot_general(
            lg_out[...], wbuf[pl.ds(at, w), :], (((1,), (1,)), ((), ())), preferred_element_type=jnp.float32
        )
        weighted = value * gain[:, pl.ds(at, w)] * sh[:, pl.ds(at, w)].astype(jnp.float32)
        inner_acc[...] += jnp.sum(weighted, axis=1, keepdims=True)
        return value

    def go_gs(b):
        return remote(sibout.at[b], sibin.at[b], gs_send.at[b], gs_recv.at[b], did(ss=1 - s))

    def order(q):
        return lax.rem(q, 2) * (q // 2) + (1 - lax.rem(q, 2)) * (V - 1 - q // 2)

    def for_sib(q):
        b = order(q)
        sibout[b] = term(b * S + 1 - s)
        go_gs(b).start()

    def for_own(q):
        b = order(q)
        part[b] = term(b * S + s)

    each(0, V, for_sib)
    each(0, V, for_own)
    inner_in[me] = jnp.transpose(jnp.broadcast_to(inner_acc[...], (frames, frames)))[0:8, :]

    def go_inner(k):
        where, other = vs_peer(k)
        return remote(inner_in.at[me], inner_in.at[me], inner_send.at[other], inner_recv.at[me], where)

    each(1, VS, lambda k: go_inner(k).start())

    def line(buf, recv, b, comes, onward):
        go_gs(b).wait_recv()
        part[b] += sibin[b]

        @pl.when(comes)
        def _():
            remote(part.at[b], buf.at[b], ln_send.at[b], recv.at[b], did(vv=onward)).wait_recv()
            part[b] += buf[b]

        remote(part.at[b], buf.at[b], ln_send.at[b], recv.at[b], did(vv=onward)).start()

    def line_step(q):
        b = V - 1 - q

        @pl.when(b > v)
        def _():
            line(rin, r_recv, b, v > 0, v + 1)

        @pl.when(q < v)
        def _():
            line(lin, l_recv, q, v < V - 1, v - 1)

    each(0, V - 1, line_step)

    def inner_wait(k):
        where, other = vs_peer(k)
        remote(inner_in.at[other], inner_in.at[other], inner_send.at[other], inner_recv.at[other], where).wait_recv()

    each(1, VS, inner_wait)
    inner_total = jnp.sum(inner_in[...], axis=0)[0:1, :]
    inner_rows = to_columns(inner_total)[:, 0:1]

    go_gs(v).wait_recv()
    part[v] += sibin[v]

    @pl.when(v > 0)
    def _():
        remote(part.at[v], rin.at[v], ln_send.at[v], r_recv.at[v], did(vv=v - 1)).wait_recv()
        part[v] += rin[v]

    @pl.when(v < V - 1)
    def _():
        remote(part.at[v], lin.at[v], ln_send.at[v], l_recv.at[v], did(vv=v + 1)).wait_recv()
        part[v] += lin[v]

    mine = pl.multiple_of(me * w, w)
    scaled = part[v] * gain[:, pl.ds(mine, w)]
    own_hidden = sh[:, pl.ds(mine, w)].astype(jnp.float32)
    hg_out[...] = (inverse * scaled - own_hidden * (inverse**3 * inner_rows / DS)).astype(jnp.bfloat16)

    def sent(i):
        o, c = i // C, lax.rem(i, C)
        here = tbuf.at[c, o * S + s]

        @pl.when((o >= v) & (v > 0))
        def _():
            go_left(o, c, here).wait_send()

        @pl.when((o <= v) & (v < V - 1))
        def _():
            go_right(o, c, here).wait_send()

        go_sib(o, c, here).wait_send()

    each(0, V * C, sent)

    def w_sent(j):
        go_x(j // CW + 1, lax.rem(j, CW)).wait_send()
        go_y(lax.rem(t + T - 1 - j // CW, T), lax.rem(j, CW)).wait_send()

    each(0, nev, w_sent)

    def acc_sent(o):
        @pl.when(o // per != t)
        def _():
            go_acc(o).wait_send()

        go_gs(o).wait_send()

        @pl.when(o > v)
        def _():
            remote(part.at[o], rin.at[o], ln_send.at[o], r_recv.at[o], did(vv=v + 1)).wait_send()

        @pl.when(o < v)
        def _():
            remote(part.at[o], lin.at[o], ln_send.at[o], l_recv.at[o], did(vv=v - 1)).wait_send()

    each(0, V, acc_sent)

    def small_sent(k):
        go_stat(k).wait_send()
        go_inner(k).wait_send()

    each(1, VS, small_sent)


def local(sizes, teacher_hidden, teacher_weight, student_hidden, student_gain, student_weight, labels, alignment, loss_mask):
    G, V, T, S, C, CW = sizes
    VS = V * S
    rows, width = teacher_hidden.shape
    fc = width // C
    N = teacher_weight.shape[1]
    frames, DS = student_hidden.shape
    w = DS // VS
    per = V // T
    f32, bf16 = jnp.float32, jnp.bfloat16
    dma = pltpu.SemaphoreType.DMA
    vmem = pl.BlockSpec(memory_space=pltpu.VMEM)
    hbm = pl.BlockSpec(memory_space=pl.ANY)
    row_loss, logit_grad, hidden_grad = pl.pallas_call(
        functools.partial(kernel, sizes),
        out_shape=(
            jax.ShapeDtypeStruct((1, frames), f32),
            jax.ShapeDtypeStruct((frames, N), bf16),
            jax.ShapeDtypeStruct((frames, w), bf16),
        ),
        in_specs=[hbm, hbm, vmem, vmem, hbm, vmem, vmem, vmem],
        out_specs=(vmem, vmem, vmem),
        scratch_shapes=[
            pltpu.VMEM((C, VS, rows, fc), bf16),
            pltpu.VMEM((C, fc, N), bf16),
            pltpu.VMEM((DS, N), bf16),
            pltpu.VMEM((frames, DS), bf16),
            pltpu.VMEM((V, S * rows, N), f32),
            pltpu.VMEM((T, per, S * rows, N), f32),
            pltpu.VMEM((frames, N), f32),
            pltpu.VMEM((VS, 8, frames), f32),
            pltpu.VMEM((VS, 8, frames), f32),
            pltpu.VMEM((V, frames, w), f32),
            pltpu.VMEM((V, frames, w), f32),
            pltpu.VMEM((V, frames, w), f32),
            pltpu.VMEM((V, frames, w), f32),
            pltpu.VMEM((V, frames, w), f32),
            pltpu.VMEM((frames, 1), f32),
            dma((C,)), dma((C,)), dma,
            dma((V, C)), dma((V, C)), dma((V, C)), dma((V, C)), dma((V, C)),
            dma((T, CW)), dma((T, CW)), dma((T, CW)), dma((T, CW)),
            dma((V,)), dma((T, per)),
            dma((VS,)), dma((VS,)), dma((VS,)), dma((VS,)),
            dma((V,)), dma((V,)), dma((V,)), dma((V,)), dma((V,)),
        ],
        compiler_params=pltpu.CompilerParams(
            collective_id=0, has_side_effects=True, vmem_limit_bytes=48 * 2**20
        ),
    )(
        teacher_hidden, teacher_weight, student_hidden, student_gain.reshape(1, DS), student_weight,
        labels.reshape(1, frames), alignment.reshape(1, frames), loss_mask.reshape(T, frames),
    )
    return row_loss.reshape(frames), logit_grad, hidden_grad


def solution(mesh):
    sizes = tuple(mesh.shape[a] for a in ("groups", "vocab", "tokens", "section")) + (4, 4)
    in_specs = (
        P(("groups", "vocab", "section"), "tokens"),
        P("tokens", ("vocab", "section")),
        P(("groups", "tokens"), None),
        P(),
        P("tokens", ("vocab", "section")),
        P(("groups", "tokens")),
        P(("groups", "tokens")),
        P("groups"),
    )
    out_specs = (
        P(("groups", "tokens")),
        P(("groups", "tokens"), ("vocab", "section")),
        P(("groups", "tokens"), ("vocab", "section")),
    )
    return jax.shard_map(
        functools.partial(local, sizes), mesh=mesh, in_specs=in_specs, out_specs=out_specs, check_vma=False
    )
```

time: 263 us -> 95.3 us (0.36)
  waiting for transfers between devices: 164 us -> 0 us
  Pallas kernels: 0 us -> 86 us
  blocking collectives: 60.6 us -> 0 us
  matrix products: 15.9 us -> 0 us
  between operations: 13.9 us -> 0.66 us
  local copies, waits for them, and re-layouts: 1.88 us -> 8.38 us
  other arithmetic: 6.31 us -> 0 us
    all_gather x2 -> x0, waiting for transfers between devices: 98.2 us -> none  [the longest x1 49.1 us: local(): full_weight = lax.all_gather(student_weight, 'tokens', axis=0, tiled=True)]
    pallas_call x0 -> x1, Pallas kernels: none -> 86 us  [local(): pl.pallas_call(functools.partial(kernel, sizes), out_shape=(jax.ShapeDtyp...]
    psum x1 -> x0, waiting for transfers between devices: 62.1 us -> none  [local(): grad_total = lax.psum(normed_grad, ('vocab', 'section'))]
    all_gather x6 -> x0, blocking collectives: 60.6 us -> none  [merged(): everything = jax.tree.map(lambda part: lax.all_gather(part, axis), shard)]
    dot_general x3 -> x0, matrix products: 15.9 us -> none  [the longest x1 7.83 us: local(): jnp.dot(lax.all_gather(teacher_hidden, ('vocab', 'section'), axis=0, tile...]
    unnamed x12 -> x17, local copies, waits for them, and re-layouts: 0.03 us -> 8.38 us
    reduce_sum x4 -> x0, other arithmetic: 3.15 us -> none  [the longest x1 1.97 us: local(): inner_rows = jnp.sum(scaled * hidden, axis=1, keepdims=True)]
  transfers between devices with their start and end apart: 4 -> 0, of which waited for: 4 -> 0; matrix products, arithmetic and copies ran while one was open for 5% -> 0% of each run, Pallas kernels for 0% -> 0%
where the time goes in v1:
time: 95.3 us; the launch traced here: 95 us
  Pallas kernels  86 us (90%)
  local copies, waits for them, and re-layouts  8.38 us (9%)
    pallas_call x1, Pallas kernels, local(): pl.pallas_call(functools.partial(kernel, sizes), out_shape=(jax.ShapeDtyp...  86 us
    unnamed x17, local copies, waits for them, and re-layouts  8.38 us

profile of v1, /device:TPU:0, one launch (start us, length us, event | category | flops | bytes accessed | tf_op | source)
XLA Modules:
  0.0 95.0 jit_solution(4845221378055772682)
XLA Ops:
  0.6 0.0 copy-start
  0.6 1.6 %copy-done = bf16[2048,512]{1,0:T(8,128)(2,1)S(1)} copy-done((bf16[2048,512]{1,0:T(8,128)(2,1)S(1)}, bf16[2048,512]{1,0:T(8,128)(2,1)}, u32[]{:S(2)}) %copy-start) | copy-done | bytes 2097176
  2.2 0.0 copy-start.1
  2.2 1.2 %copy-done.1 = bf16[128,4096]{1,0:T(8,128)(2,1)S(1)} copy-done((bf16[128,4096]{1,0:T(8,128)(2,1)S(1)}, bf16[128,4096]{1,0:T(8,128)(2,1)}, u32[]{:S(2)}) %copy-start.1) | copy-done | bytes 1048600
  3.5 0.0 copy-start.2
  3.5 1.0 %copy-done.2 = bf16[32,8192]{1,0:T(8,128)(2,1)S(1)} copy-done((bf16[32,8192]{1,0:T(8,128)(2,1)S(1)}, bf16[32,8192]{1,0:T(8,128)(2,1)}, u32[]{:S(2)}) %copy-start.2) | copy-done | bytes 524312
  4.5 0.0 copy-start.3
  4.5 0.7 copy-done.3
  5.2 0.0 copy-start.4
  5.2 0.7 copy-done.4
  5.9 0.0 copy-start.5
  5.9 0.7 copy-done.5
  6.5 0.0 copy-start.6
  6.5 0.7 copy-done.6
  7.2 86.0 %shard_map.103 = (f32[1,128]{1,0:T(1,128)S(1)}, bf16[128,512]{1,0:T(8,128)(2,1)S(1)}, bf16[128,512]{1,0:T(8,128)(2,1)S(1)}) custom-call(bf16[32,8192]{1,0:T(8,128)(2,1)S(1)} %copy-done.2, bf16[8192,512]{1,0:T(8,128)(2,1)} %tw.1, bf16[128,4096]{1,0:T(8,128)(2,1)S(1)} %copy-done.1, f32[1,4096]{1,0:T(1,128)S(1)} %bitcast.5, bf16[2048,512]{1,0:T(8,128)(2,1)S(1)} %copy-done, ...), custom_call_target="tpu_custom_call" | custom-call | tf_op jit(solution)/shard_map/pallas_call | solution.py:443
  93.2 0.5 copy.14
  93.7 0.7 copy.15
  94.3 0.7 copy.16
Async XLA Ops:
  0.6 1.6 %copy-start = (bf16[2048,512]{1,0:T(8,128)(2,1)S(1)}, bf16[2048,512]{1,0:T(8,128)(2,1)}, u32[]{:S(2)}) copy-start(bf16[2048,512]{1,0:T(8,128)(2,1)} %sw.1) | copy-start | bytes 6291460
  2.2 1.2 %copy-start.1 = (bf16[128,4096]{1,0:T(8,128)(2,1)S(1)}, bf16[128,4096]{1,0:T(8,128)(2,1)}, u32[]{:S(2)}) copy-start(bf16[128,4096]{1,0:T(8,128)(2,1)} %sh.1) | copy-start | bytes 3145732
  3.5 1.0 %copy-start.2 = (bf16[32,8192]{1,0:T(8,128)(2,1)S(1)}, bf16[32,8192]{1,0:T(8,128)(2,1)}, u32[]{:S(2)}) copy-start(bf16[32,8192]{1,0:T(8,128)(2,1)} %th.1) | copy-start | bytes 1572868
  4.5 0.7 copy-start.3
  5.2 0.7 copy-start.4
  5.9 0.7 copy-start.5
  6.5 0.7 copy-start.6

commit v2 on v1

--- a/solution.py
+++ b/solution.py
@@ -14,17 +14,18 @@
 
 
 def kernel(
-    sizes, th, tw, sh, gain, sw, labels, align, mask,
-    rl_out, lg_out, hg_out,
+    sizes, th, tw, sh_in, gain_in, sw, labels_in, align_in, mask_in,
+    rl_hbm, lg_hbm, hg_hbm,
+    sh, gain, labels, align, mask, rl_out, lg_out, hg_out,
     tbuf, twv, wbuf, normed, acc, tin, bl, stats, inner_in, sibout, sibin, part, rin, lin, inner_acc,
-    tw_sem, own_sem, sw_sem,
+    tw_sem, own_sem, sw_sem, in_sem, out_sem,
     left_send, right_send, sib_send, z_recv, s_recv,
     x_send, x_recv, y_send, y_recv,
     acc_send, acc_recv,
     stat_send, stat_recv, inner_send, inner_recv,
     gs_send, gs_recv, ln_send, r_recv, l_recv,
 ):
-    G, V, T, S, C, CW = sizes
+    G, V, T, S, C, CW, RP, WIN, LAG = sizes
     VS = V * S
     g, v, t, s = (lax.axis_index(a) for a in ("groups", "vocab", "tokens", "section"))
     me = v * S + s
@@ -37,6 +38,7 @@
     N = tw.shape[1]
     w = DS // VS
     per = V // T
+    rp = frames // RP
 
     def did(gg=None, vv=None, tt=None, ss=None):
         pick = lambda a, b: b if a is None else a
@@ -63,6 +65,14 @@
     def greet(where):
         pl.semaphore_signal(barrier, inc=1, device_id=where, device_id_type=MESH)
 
+    loads = [
+        pltpu.make_async_copy(source, target, in_sem.at[i])
+        for i, (source, target) in enumerate(
+            ((sh_in, sh), (gain_in, gain), (labels_in, labels), (align_in, align), (mask_in, mask))
+        )
+    ]
+    for load in loads:
+        load.start()
     for c in range(C):
         pltpu.make_async_copy(tw.at[c * fc:(c + 1) * fc], twv.at[c], tw_sem.at[c]).start()
         pltpu.make_async_copy(th.at[:, c * fc:(c + 1) * fc], tbuf.at[c, me], own_sem.at[c]).start()
@@ -122,6 +132,8 @@
         x_wait(tt, cw)
         go_y(tt, cw).start()
 
+    for load in loads:
+        load.wait()
     hid = sh[...].astype(jnp.float32)
     inverse = lax.rsqrt(jnp.mean(hid * hid, axis=1, keepdims=True) + epsilon)
     normed[...] = (hid * inverse * gain[...]).astype(jnp.bfloat16)
@@ -294,6 +306,12 @@
         * ((1.0 + label_weight) * student_prob - teacher_prob - label_weight * onehot.astype(jnp.float32))
     ).astype(jnp.bfloat16)
     lg_out[...] = grad
+    stores = [
+        pltpu.make_async_copy(source, target, out_sem.at[i])
+        for i, (source, target) in enumerate(((rl_out, rl_hbm), (lg_out, lg_hbm), (hg_out, hg_hbm)))
+    ]
+    stores[0].start()
+    stores[1].start()
 
     inner_acc[...] = jnp.zeros_like(inner_acc)
 
@@ -331,29 +349,49 @@
 
     each(1, VS, lambda k: go_inner(k).start())
 
-    def line(buf, recv, b, comes, onward):
-        go_gs(b).wait_recv()
-        part[b] += sibin[b]
+    def piece(buf, b, p):
+        return buf.at[b, pl.ds(pl.multiple_of(p * rp, rp), rp)]
+
+    def go_line(buf, recv, b, p, onward):
+        return remote(piece(part, b, p), piece(buf, b, p), ln_send.at[b, p], recv.at[b, p], did(vv=onward))
+
+    def line(n, buf, recv, b_of, comes, onward):
+        q, p = n // RP, lax.rem(n, RP)
+        b = b_of(q)
+
+        @pl.when(p == 0)
+        def _():
+            go_gs(b).wait_recv()
+            part[b] += sibin[b]
 
         @pl.when(comes)
         def _():
-            remote(part.at[b], buf.at[b], ln_send.at[b], recv.at[b], did(vv=onward)).wait_recv()
-            part[b] += buf[b]
-
-        remote(part.at[b], buf.at[b], ln_send.at[b], recv.at[b], did(vv=onward)).start()
-
-    def line_step(q):
-        b = V - 1 - q
-
-        @pl.when(b > v)
-        def _():
-            line(rin, r_recv, b, v > 0, v + 1)
-
-        @pl.when(q < v)
-        def _():
-            line(lin, l_recv, q, v < V - 1, v - 1)
-
-    each(0, V - 1, line_step)
+            at = pl.ds(pl.multiple_of(p * rp, rp), rp)
+            go_line(buf, recv, b, p, onward).wait_recv()
+            part[b, at] += buf[b, at]
+
+        @pl.when(n >= WIN)
+        def _():
+            go_line(buf, recv, b_of((n - WIN) // RP), lax.rem(n - WIN, RP), onward).wait_send()
+
+        go_line(buf, recv, b, p, onward).start()
+
+    from_top, from_zero = (lambda q: V - 1 - q), (lambda q: q)
+
+    def line_step(i):
+        n = i - v * LAG
+
+        @pl.when((n >= 0) & (n < (V - 1 - v) * RP))
+        def _():
+            line(n, rin, r_recv, from_top, v > 0, v + 1)
+
+        m = i - (V - 1 - v) * LAG
+
+        @pl.when((m >= 0) & (m < v * RP))
+        def _():
+            line(m, lin, l_recv, from_zero, v < V - 1, v - 1)
+
+    each(0, (V - 1) * max(RP, LAG), line_step)
 
     def inner_wait(k):
         where, other = vs_peer(k)
@@ -366,21 +404,25 @@
     go_gs(v).wait_recv()
     part[v] += sibin[v]
 
+    def last(buf, recv, onward):
+        each(0, RP, lambda p: go_line(buf, recv, v, p, onward).wait_recv())
+        part[v] += buf[v]
+
     @pl.when(v > 0)
     def _():
-        remote(part.at[v], rin.at[v], ln_send.at[v], r_recv.at[v], did(vv=v - 1)).wait_recv()
-        part[v] += rin[v]
+        last(rin, r_recv, v - 1)
 
     @pl.when(v < V - 1)
     def _():
-        remote(part.at[v], lin.at[v], ln_send.at[v], l_recv.at[v], did(vv=v + 1)).wait_recv()
-        part[v] += lin[v]
+        last(lin, l_recv, v + 1)
 
     mine = pl.multiple_of(me * w, w)
     scaled = part[v] * gain[:, pl.ds(mine, w)]
     own_hidden = sh[:, pl.ds(mine, w)].astype(jnp.float32)
     hg_out[...] = (inverse * scaled - own_hidden * (inverse**3 * inner_rows / DS)).astype(jnp.bfloat16)
 
+    stores[2].start()
+
     def sent(i):
         o, c = i // C, lax.rem(i, C)
         here = tbuf.at[c, o * S + s]
@@ -410,14 +452,18 @@
 
         go_gs(o).wait_send()
 
-        @pl.when(o > v)
-        def _():
-            remote(part.at[o], rin.at[o], ln_send.at[o], r_recv.at[o], did(vv=v + 1)).wait_send()
-
-        @pl.when(o < v)
-        def _():
-            remote(part.at[o], lin.at[o], ln_send.at[o], l_recv.at[o], did(vv=v - 1)).wait_send()
-
+    def line_sent(j):
+        @pl.when(v < V - 1)
+        def _():
+            n = (V - 1 - v) * RP - WIN + j
+            go_line(rin, r_recv, from_top(n // RP), lax.rem(n, RP), v + 1).wait_send()
+
+        @pl.when(v > 0)
+        def _():
+            n = v * RP - WIN + j
+            go_line(lin, l_recv, n // RP, lax.rem(n, RP), v - 1).wait_send()
+
+    each(0, WIN, line_sent)
     each(0, V, acc_sent)
 
     def small_sent(k):
@@ -425,10 +471,12 @@
         go_inner(k).wait_send()
 
     each(1, VS, small_sent)
+    for store in stores:
+        store.wait()
 
 
 def local(sizes, teacher_hidden, teacher_weight, student_hidden, student_gain, student_weight, labels, alignment, loss_mask):
-    G, V, T, S, C, CW = sizes
+    G, V, T, S, C, CW, RP, WIN, LAG = sizes
     VS = V * S
     rows, width = teacher_hidden.shape
     fc = width // C
@@ -438,7 +486,6 @@
     per = V // T
     f32, bf16 = jnp.float32, jnp.bfloat16
     dma = pltpu.SemaphoreType.DMA
-    vmem = pl.BlockSpec(memory_space=pltpu.VMEM)
     hbm = pl.BlockSpec(memory_space=pl.ANY)
     row_loss, logit_grad, hidden_grad = pl.pallas_call(
         functools.partial(kernel, sizes),
@@ -447,9 +494,17 @@
             jax.ShapeDtypeStruct((frames, N), bf16),
             jax.ShapeDtypeStruct((frames, w), bf16),
         ),
-        in_specs=[hbm, hbm, vmem, vmem, hbm, vmem, vmem, vmem],
-        out_specs=(vmem, vmem, vmem),
+        in_specs=[hbm] * 8,
+        out_specs=(hbm, hbm, hbm),
         scratch_shapes=[
+            pltpu.VMEM((frames, DS), bf16),
+            pltpu.VMEM((1, DS), f32),
+            pltpu.VMEM((1, frames), jnp.int32),
+            pltpu.VMEM((1, frames), jnp.int32),
+            pltpu.VMEM((T, frames), jnp.int32),
+            pltpu.VMEM((1, frames), f32),
+            pltpu.VMEM((frames, N), bf16),
+            pltpu.VMEM((frames, w), bf16),
             pltpu.VMEM((C, VS, rows, fc), bf16),
             pltpu.VMEM((C, fc, N), bf16),
             pltpu.VMEM((DS, N), bf16),
@@ -465,15 +520,15 @@
             pltpu.VMEM((V, frames, w), f32),
             pltpu.VMEM((V, frames, w), f32),
             pltpu.VMEM((frames, 1), f32),
-            dma((C,)), dma((C,)), dma,
+            dma((C,)), dma((C,)), dma, dma((5,)), dma((3,)),
             dma((V, C)), dma((V, C)), dma((V, C)), dma((V, C)), dma((V, C)),
             dma((T, CW)), dma((T, CW)), dma((T, CW)), dma((T, CW)),
             dma((V,)), dma((T, per)),
             dma((VS,)), dma((VS,)), dma((VS,)), dma((VS,)),
-            dma((V,)), dma((V,)), dma((V,)), dma((V,)), dma((V,)),
+            dma((V,)), dma((V,)), dma((V, RP)), dma((V, RP)), dma((V, RP)),
         ],
         compiler_params=pltpu.CompilerParams(
-            collective_id=0, has_side_effects=True, vmem_limit_bytes=48 * 2**20
+            collective_id=0, has_side_effects=True, vmem_limit_bytes=63 * 2**20
         ),
     )(
         teacher_hidden, teacher_weight, student_hidden, student_gain.reshape(1, DS), student_weight,
@@ -483,7 +538,7 @@
 
 
 def solution(mesh):
-    sizes = tuple(mesh.shape[a] for a in ("groups", "vocab", "tokens", "section")) + (4, 4)
+    sizes = tuple(mesh.shape[a] for a in ("groups", "vocab", "tokens", "section")) + (4, 4, 4, 2, 2)
     in_specs = (
         P(("groups", "vocab", "section"), "tokens"),
         P("tokens", ("vocab", "section")),

time: 95.3 us -> 80 us (0.84)
  Pallas kernels: 86 us -> 74.8 us
  local copies, waits for them, and re-layouts: 8.38 us -> 4.26 us
    pallas_call x1, Pallas kernels: 86 us -> 74.8 us  [local(): pl.pallas_call(functools.partial(kernel, sizes), out_shape=(jax.ShapeDtyp...]
    unnamed x17 -> x3, local copies, waits for them, and re-layouts: 8.38 us -> 4.26 us
where the time goes in v2:
time: 80 us; the launch traced here: 79.7 us
  Pallas kernels  74.8 us (94%)
  local copies, waits for them, and re-layouts  4.26 us (5%)
    pallas_call x1, Pallas kernels, local(): pl.pallas_call(functools.partial(kernel, sizes), out_shape=(jax.ShapeDtyp...  74.8 us
    unnamed x3, local copies, waits for them, and re-layouts  4.26 us

profile of v2, /device:TPU:0, one launch (start us, length us, event | category | flops | bytes accessed | tf_op | source)
XLA Modules:
  0.0 79.7 jit_solution(1603580933049911633)
XLA Ops:
  0.6 74.8 %shard_map.103 = (f32[1,128]{1,0:T(1,128)}, bf16[128,512]{1,0:T(8,128)(2,1)}, bf16[128,512]{1,0:T(8,128)(2,1)}) custom-call(bf16[32,8192]{1,0:T(8,128)(2,1)} %th.1, bf16[8192,512]{1,0:T(8,128)(2,1)} %tw.1, bf16[128,4096]{1,0:T(8,128)(2,1)} %sh_in.1, f32[1,4096]{1,0:T(1,128)} %bitcast.5, bf16[2048,512]{1,0:T(8,128)(2,1)} %sw.1, s32[1,128]{1,0:T(1,128)} %bitcast.7, ...), custom_call_target="tpu_custom_call" | custom-call | tf_op jit(solution)/shard_map/pallas_call | solution.py:490
  75.4 1.1 %copy.14 = f32[128]{0:T(128)} copy(f32[128]{0:T(128)} %bitcast.9) | data formatting | bytes 1024
  76.5 1.6 %copy.15 = bf16[128,512]{1,0:T(8,128)(2,1)} copy(bf16[128,512]{1,0:T(8,128)(2,1)} %get-tuple-element.13) | data formatting | bytes 262144
  78.1 1.6 %copy.16 = bf16[128,512]{1,0:T(8,128)(2,1)} copy(bf16[128,512]{1,0:T(8,128)(2,1)} %get-tuple-element.14) | data formatting | bytes 262144

commit v3 on v2

--- a/solution.py
+++ b/solution.py
@@ -15,7 +15,7 @@
 
 def kernel(
     sizes, th, tw, sh_in, gain_in, sw, labels_in, align_in, mask_in,
-    rl_hbm, lg_hbm, hg_hbm,
+    rl_hbm, out_hbm,
     sh, gain, labels, align, mask, rl_out, lg_out, hg_out,
     tbuf, twv, wbuf, normed, acc, tin, bl, stats, inner_in, sibout, sibin, part, rin, lin, inner_acc,
     tw_sem, own_sem, sw_sem, in_sem, out_sem,
@@ -308,7 +308,11 @@
     lg_out[...] = grad
     stores = [
         pltpu.make_async_copy(source, target, out_sem.at[i])
-        for i, (source, target) in enumerate(((rl_out, rl_hbm), (lg_out, lg_hbm), (hg_out, hg_hbm)))
+        for i, (source, target) in enumerate((
+            (rl_out, rl_hbm),
+            (lg_out, out_hbm.at[:, 0:N]),
+            (hg_out, out_hbm.at[:, N:]),
+        ))
     ]
     stores[0].start()
     stores[1].start()
@@ -339,8 +343,53 @@
         b = order(q)
         part[b] = term(b * S + s)
 
-    each(0, V, for_sib)
-    each(0, V, for_own)
+    def piece(buf, b, p):
+        return buf.at[b, pl.ds(pl.multiple_of(p * rp, rp), rp)]
+
+    def go_line(buf, recv, b, p, onward):
+        return remote(piece(part, b, p), piece(buf, b, p), ln_send.at[b, p], recv.at[b, p], did(vv=onward))
+
+    def line(n, buf, recv, b_of, comes, onward):
+        q, p = n // RP, lax.rem(n, RP)
+        b = b_of(q)
+
+        @pl.when(p == 0)
+        def _():
+            go_gs(b).wait_recv()
+            part[b] += sibin[b]
+
+        @pl.when(comes)
+        def _():
+            at = pl.ds(pl.multiple_of(p * rp, rp), rp)
+            go_line(buf, recv, b, p, onward).wait_recv()
+            part[b, at] += buf[b, at]
+
+        @pl.when(n >= WIN)
+        def _():
+            go_line(buf, recv, b_of((n - WIN) // RP), lax.rem(n - WIN, RP), onward).wait_send()
+
+        go_line(buf, recv, b, p, onward).start()
+
+    from_top, from_zero = (lambda q: V - 1 - q), (lambda q: q)
+
+    def line_step(i):
+        n = i - v * LAG
+
+        @pl.when((n >= 0) & (n < (V - 1 - v) * RP))
+        def _():
+            line(n, rin, r_recv, from_top, v > 0, v + 1)
+
+        m = i - (V - 1 - v) * LAG
+
+        @pl.when((m >= 0) & (m < v * RP))
+        def _():
+            line(m, lin, l_recv, from_zero, v < V - 1, v - 1)
+
+    each(0, 2, for_sib)
+    each(0, 2, for_own)
+    each(0, LAG, line_step)
+    each(2, V, for_sib)
+    each(2, V, for_own)
     inner_in[me] = jnp.transpose(jnp.broadcast_to(inner_acc[...], (frames, frames)))[0:8, :]
 
     def go_inner(k):
@@ -348,50 +397,7 @@
         return remote(inner_in.at[me], inner_in.at[me], inner_send.at[other], inner_recv.at[me], where)
 
     each(1, VS, lambda k: go_inner(k).start())
-
-    def piece(buf, b, p):
-        return buf.at[b, pl.ds(pl.multiple_of(p * rp, rp), rp)]
-
-    def go_line(buf, recv, b, p, onward):
-        return remote(piece(part, b, p), piece(buf, b, p), ln_send.at[b, p], recv.at[b, p], did(vv=onward))
-
-    def line(n, buf, recv, b_of, comes, onward):
-        q, p = n // RP, lax.rem(n, RP)
-        b = b_of(q)
-
-        @pl.when(p == 0)
-        def _():
-            go_gs(b).wait_recv()
-            part[b] += sibin[b]
-
-        @pl.when(comes)
-        def _():
-            at = pl.ds(pl.multiple_of(p * rp, rp), rp)
-            go_line(buf, recv, b, p, onward).wait_recv()
-            part[b, at] += buf[b, at]
-
-        @pl.when(n >= WIN)
-        def _():
-            go_line(buf, recv, b_of((n - WIN) // RP), lax.rem(n - WIN, RP), onward).wait_send()
-
-        go_line(buf, recv, b, p, onward).start()
-
-    from_top, from_zero = (lambda q: V - 1 - q), (lambda q: q)
-
-    def line_step(i):
-        n = i - v * LAG
-
-        @pl.when((n >= 0) & (n < (V - 1 - v) * RP))
-        def _():
-            line(n, rin, r_recv, from_top, v > 0, v + 1)
-
-        m = i - (V - 1 - v) * LAG
-
-        @pl.when((m >= 0) & (m < v * RP))
-        def _():
-            line(m, lin, l_recv, from_zero, v < V - 1, v - 1)
-
-    each(0, (V - 1) * max(RP, LAG), line_step)
+    each(LAG, (V - 1) * max(RP, LAG), line_step)
 
     def inner_wait(k):
         where, other = vs_peer(k)
@@ -487,15 +493,11 @@
     f32, bf16 = jnp.float32, jnp.bfloat16
     dma = pltpu.SemaphoreType.DMA
     hbm = pl.BlockSpec(memory_space=pl.ANY)
-    row_loss, logit_grad, hidden_grad = pl.pallas_call(
+    row_loss, both = pl.pallas_call(
         functools.partial(kernel, sizes),
-        out_shape=(
-            jax.ShapeDtypeStruct((1, frames), f32),
-            jax.ShapeDtypeStruct((frames, N), bf16),
-            jax.ShapeDtypeStruct((frames, w), bf16),
-        ),
+        out_shape=(jax.ShapeDtypeStruct((1, frames), f32), jax.ShapeDtypeStruct((frames, N + w), bf16)),
         in_specs=[hbm] * 8,
-        out_specs=(hbm, hbm, hbm),
+        out_specs=(hbm, hbm),
         scratch_shapes=[
             pltpu.VMEM((frames, DS), bf16),
             pltpu.VMEM((1, DS), f32),
@@ -534,7 +536,7 @@
         teacher_hidden, teacher_weight, student_hidden, student_gain.reshape(1, DS), student_weight,
         labels.reshape(1, frames), alignment.reshape(1, frames), loss_mask.reshape(T, frames),
     )
-    return row_loss.reshape(frames), logit_grad, hidden_grad
+    return row_loss.reshape(frames), both[:, :N], both[:, N:]
 
 
 def solution(mesh):

time: 80 us -> 77.1 us (0.964)
  Pallas kernels: 74.8 us -> 73.3 us
  local copies, waits for them, and re-layouts: 4.26 us -> 2.77 us
    unnamed x3 -> x1, local copies, waits for them, and re-layouts: 4.26 us -> 1.08 us
    slice x0 -> x1, local copies, waits for them, and re-layouts: none -> 1.68 us  [local(): return (row_loss.reshape(frames), both[:, :N], both[:, N:])]
    pallas_call x1, Pallas kernels: 74.8 us -> 73.3 us  [local(): pl.pallas_call(functools.partial(kernel, sizes), out_shape=(jax.ShapeDtyp...]
where the time goes in v3:
time: 77.1 us; the launch traced here: 76.7 us
  Pallas kernels  73.3 us (95%)
  local copies, waits for them, and re-layouts  2.77 us (4%)
    pallas_call x1, Pallas kernels, local(): pl.pallas_call(functools.partial(kernel, sizes), out_shape=(jax.ShapeDtyp...  73.3 us
    slice x1, local copies, waits for them, and re-layouts, local(): return (row_loss.reshape(frames), both[:, :N], both[:, N:])  1.68 us

profile of v3, /device:TPU:0, one launch (start us, length us, event | category | flops | bytes accessed | tf_op | source)
XLA Modules:
  0.0 76.7 jit_solution(10745238917362991358)
XLA Ops:
  0.6 73.3 %shard_map.103 = (f32[1,128]{1,0:T(1,128)}, bf16[128,1024]{1,0:T(8,128)(2,1)}) custom-call(bf16[32,8192]{1,0:T(8,128)(2,1)} %th.1, bf16[8192,512]{1,0:T(8,128)(2,1)} %tw.1, bf16[128,4096]{1,0:T(8,128)(2,1)} %sh_in.1, f32[1,4096]{1,0:T(1,128)} %bitcast.5, bf16[2048,512]{1,0:T(8,128)(2,1)} %sw.1, s32[1,128]{1,0:T(1,128)} %bitcast.7, s32[1,128]{1,0:T(1,128)} %bitcast.8, ...), custom_call_target="tpu_custom_call" | custom-call | tf_op jit(solution)/shard_map/pallas_call | solution.py:496
  73.9 1.7 %fusion = (bf16[128,512]{1,0:T(8,128)(2,1)}, bf16[128,512]{1,0:T(8,128)(2,1)}) fusion(bf16[128,1024]{1,0:T(8,128)(2,1)} %get-tuple-element.6), kind=kLoop, calls=%fused_computation | loop fusion | bytes 524288 | tf_op jit(solution)/shard_map/slice | solution.py:539
  75.6 1.1 %copy.12 = f32[128]{0:T(128)} copy(f32[128]{0:T(128)} %bitcast.9) | data formatting | bytes 1024

commit v4 on v3

--- a/solution.py
+++ b/solution.py
@@ -403,6 +403,42 @@
         where, other = vs_peer(k)
         remote(inner_in.at[other], inner_in.at[other], inner_send.at[other], inner_recv.at[other], where).wait_recv()
 
+    def sent(i):
+        o, c = i // C, lax.rem(i, C)
+        here = tbuf.at[c, o * S + s]
+
+        @pl.when((o >= v) & (v > 0))
+        def _():
+            go_left(o, c, here).wait_send()
+
+        @pl.when((o <= v) & (v < V - 1))
+        def _():
+            go_right(o, c, here).wait_send()
+
+        go_sib(o, c, here).wait_send()
+
+    each(0, V * C, sent)
+
+    def w_sent(j):
+        go_x(j // CW + 1, lax.rem(j, CW)).wait_send()
+        go_y(lax.rem(t + T - 1 - j // CW, T), lax.rem(j, CW)).wait_send()
+
+    each(0, nev, w_sent)
+
+    def acc_sent(o):
+        @pl.when(o // per != t)
+        def _():
+            go_acc(o).wait_send()
+
+        go_gs(o).wait_send()
+
+    each(0, V, acc_sent)
+
+    def small_sent(k):
+        go_stat(k).wait_send()
+        go_inner(k).wait_send()
+
+    each(1, VS, small_sent)
     each(1, VS, inner_wait)
     inner_total = jnp.sum(inner_in[...], axis=0)[0:1, :]
     inner_rows = to_columns(inner_total)[:, 0:1]
@@ -429,35 +465,6 @@
 
     stores[2].start()
 
-    def sent(i):
-        o, c = i // C, lax.rem(i, C)
-        here = tbuf.at[c, o * S + s]
-
-        @pl.when((o >= v) & (v > 0))
-        def _():
-            go_left(o, c, here).wait_send()
-
-        @pl.when((o <= v) & (v < V - 1))
-        def _():
-            go_right(o, c, here).wait_send()
-
-        go_sib(o, c, here).wait_send()
-
-    each(0, V * C, sent)
-
-    def w_sent(j):
-        go_x(j // CW + 1, lax.rem(j, CW)).wait_send()
-        go_y(lax.rem(t + T - 1 - j // CW, T), lax.rem(j, CW)).wait_send()
-
-    each(0, nev, w_sent)
-
-    def acc_sent(o):
-        @pl.when(o // per != t)
-        def _():
-            go_acc(o).wait_send()
-
-        go_gs(o).wait_send()
-
     def line_sent(j):
         @pl.when(v < V - 1)
         def _():
@@ -470,13 +477,6 @@
             go_line(lin, l_recv, n // RP, lax.rem(n, RP), v - 1).wait_send()
 
     each(0, WIN, line_sent)
-    each(0, V, acc_sent)
-
-    def small_sent(k):
-        go_stat(k).wait_send()
-        go_inner(k).wait_send()
-
-    each(1, VS, small_sent)
     for store in stores:
         store.wait()
 

time: 77.1 us -> 77.1 us (level)
  no operation moved by 1% of the time
where the time goes in v4:
time: 77.1 us; the launch traced here: 76.6 us
  Pallas kernels  73.2 us (95%)
  local copies, waits for them, and re-layouts  2.77 us (4%)
    pallas_call x1, Pallas kernels, local(): pl.pallas_call(functools.partial(kernel, sizes), out_shape=(jax.ShapeDtyp...  73.2 us
    slice x1, local copies, waits for them, and re-layouts, local(): return (row_loss.reshape(frames), both[:, :N], both[:, N:])  1.68 us

profile of v4, /device:TPU:0, one launch (start us, length us, event | category | flops | bytes accessed | tf_op | source)
XLA Modules:
  0.0 76.6 jit_solution(10111168481054357997)
XLA Ops:
  0.6 73.2 %shard_map.103 = (f32[1,128]{1,0:T(1,128)}, bf16[128,1024]{1,0:T(8,128)(2,1)}) custom-call(bf16[32,8192]{1,0:T(8,128)(2,1)} %th.1, bf16[8192,512]{1,0:T(8,128)(2,1)} %tw.1, bf16[128,4096]{1,0:T(8,128)(2,1)} %sh_in.1, f32[1,4096]{1,0:T(1,128)} %bitcast.5, bf16[2048,512]{1,0:T(8,128)(2,1)} %sw.1, s32[1,128]{1,0:T(1,128)} %bitcast.7, s32[1,128]{1,0:T(1,128)} %bitcast.8, ...), custom_call_target="tpu_custom_call" | custom-call | tf_op jit(solution)/shard_map/pallas_call | solution.py:496
  73.9 1.7 %fusion = (bf16[128,512]{1,0:T(8,128)(2,1)}, bf16[128,512]{1,0:T(8,128)(2,1)}) fusion(bf16[128,1024]{1,0:T(8,128)(2,1)} %get-tuple-element.6), kind=kLoop, calls=%fused_computation | loop fusion | bytes 524288 | tf_op jit(solution)/shard_map/slice | solution.py:539
  75.6 1.1 %copy.12 = f32[128]{0:T(128)} copy(f32[128]{0:T(128)} %bitcast.9) | data formatting | bytes 1024
